TPU v7x, 32 devices: a whole 2x2x4 slice. The times are simulated.
32 devices in a mesh: dp: 4 (over y, core), expert: 8 (over z, x).
Axes of the slice: x: 2, y: 2, z: 4, core: 2. Of those that a mesh axis runs over, the one named last changes fastest.
Arguments:
- tokens: bfloat16 [8, 16, 4096], P('expert', None, 'dp'), may hold values from -6 to 6
- routes: int32 [8, 16, 8], P('expert'), may hold values from 0 to 7, all different within a row; in each aligned block of 16 rows (0 to 15, 16 to 31, ..., all dimensions but the last counted through in order) at most 16 rows name the same one
- gates: float32 [8, 16, 8], P('expert'), may hold values from 0.05 to 0.3
- plan: int32 [8], replicated, may hold values from 0 to 7, each once
- proj_weight: bfloat16 [8, 2, 4096, 768], P('expert', None, 'dp'), may hold values from -0.09375 to 0.09375
- proj_grad: bfloat16 [8, 2, 4096, 768], P('expert', None, 'dp'), may hold values from -6 to 6
- first_moment: float32 [8, 2, 4096, 768], P('expert', None, 'dp'), may hold values from -1.8 to 1.8
- second_moment: float32 [8, 2, 4096, 768], P('expert', None, 'dp'), may hold values from 0.01 to 0.1
- down_weight: bfloat16 [8, 768, 4096], P('expert', None, 'dp'), may hold values from -0.21875 to 0.21875
Outputs:
- out_tokens: bfloat16 [8, 16, 4096], P('expert', None, 'dp')
- new_proj: bfloat16 [8, 2, 4096, 768], P('expert', None, 'dp')
- new_down: bfloat16 [8, 768, 4096], P('expert', None, 'dp')
Inputs may be any that keep to these rules, and one draw needn't show every extreme that they name: `routes`: each token names 8 different experts; within one group no expert is named by more than 16 tokens, and in some group some expert is named by exactly 16. Expert x moves to the owner plan[x]; every owner receives exactly one expert.
All inputs are finite; a program needn't handle non-finite values.
Results may differ from a plain program's by a relative error of at most 0.024.
Values may be sent and summed in bfloat16 or wider, within the bound.
A program may use at most 64 MiB of HBM per device.

v0:
```python
import itertools

import jax
import jax.numpy as jnp
import numpy as np
from jax import lax
from jax.sharding import PartitionSpec as P

learning_rate = 0.01
beta_first = 0.9
beta_second = 0.999
adam_epsilon = 1e-08
bias_first = 1.0 - 0.9**10
bias_second = 1.0 - 0.999**10


def adam_update(weights, grads, first_moment, second_moment):
    grad_float = grads.astype(jnp.float32)
    first_new = beta_first * first_moment + (1.0 - beta_first) * grad_float
    second_new = beta_second * second_moment + (1.0 - beta_second) * grad_float * grad_float
    adam_step = first_new / bias_first / (jnp.sqrt(second_new / bias_second) + adam_epsilon)
    return (weights.astype(jnp.float32) - learning_rate * adam_step).astype(jnp.bfloat16)


max_levels = 4


def partial_products(slots, pieces):
    total, start = 0.0, 0
    for updated in pieces:
        rows = updated.shape[1]
        joined = jnp.concatenate([updated[0], updated[1]], axis=1)
        total += jnp.dot(
            slots[:, start : start + rows], joined, preferred_element_type=jnp.float32
        )
        start += rows
    return total.astype(jnp.bfloat16)


def dp_blocks(partials):
    parts = lax.axis_size("dp")
    return lax.all_to_all(
        partials.reshape(1, parts, -1, partials.shape[1]),
        "dp",
        split_axis=1,
        concat_axis=1,
        tiled=True,
    )


def finish_rows(blocks, down_local):
    width = down_local.shape[0]
    summed = jnp.sum(blocks[0].astype(jnp.float32), axis=0)
    hidden = (jax.nn.silu(summed[:, :width]) * summed[:, width:]).astype(jnp.bfloat16)
    result = jnp.dot(
        lax.all_gather(hidden, "dp", axis=0, tiled=True),
        down_local,
        preferred_element_type=jnp.float32,
    )
    return result.astype(jnp.bfloat16)


def owner_exchange(pieces):
    return lax.all_to_all(pieces, "expert", split_axis=1, concat_axis=1, tiled=True)


def two_phase_migration(plan, updated, down_local):
    owners = lax.axis_size("expert")
    local_rows, width = updated.shape[1:]
    expert_ids = jnp.arange(owners, dtype=jnp.int32)
    spread_down = owner_exchange(down_local.reshape(1, owners, width // owners, local_rows))
    spread_proj = owner_exchange(updated.reshape(2, owners, local_rows // owners, width))
    inverse = jnp.sum(
        jnp.where(plan[None, :] == expert_ids[:, None], expert_ids[None, :], 0), axis=1
    )
    moved_down = owner_exchange(jnp.take(spread_down, inverse, axis=1))
    moved_proj = owner_exchange(jnp.take(spread_proj, inverse, axis=1))
    return moved_proj.reshape(2, local_rows, width), moved_down.reshape(width, local_rows)


def colour_table(levels):
    bits = np.array(list(itertools.product((0, 1), repeat=levels)), np.int32)
    return np.stack([bits, 1 - bits], axis=2).reshape(len(bits), 2 * levels)


def worst_cut(perm):
    worst = 0
    for cut in range(1, len(perm)):
        up = sum(1 for z, to in enumerate(perm) if z < cut <= to)
        worst = max(worst, up)
    return worst


def route_choice(plan, levels):
    owners = 2 * levels
    perms = list(itertools.permutations(range(levels)))
    colours = colour_table(levels)
    ids = jnp.arange(owners, dtype=jnp.int32)
    arrives = plan[:, None] == ids[None, :]
    landed = jnp.sum(jnp.where(arrives[None], colours[:, :, None], 0), axis=1)
    pair_sum = landed.reshape(-1, levels, 2).sum(axis=2)
    bad = jnp.sum((pair_sum != 1).astype(jnp.int32), axis=1)
    scale = np.repeat(levels ** np.arange(levels, dtype=np.int32), 2)
    term = (plan // 2) * scale
    codes = np.array([sum(to * levels**z for z, to in enumerate(p)) for p in perms], np.int32)
    costs = np.array([worst_cut(p) for p in perms], np.int32)
    keys = [
        jnp.sum(jnp.where(colours == colour, term[None, :], 0), axis=1) for colour in (0, 1)
    ]
    hits = [key[:, None] == codes[None, :] for key in keys]
    cost = sum(jnp.sum(jnp.where(hit, costs[None, :], 0), axis=1) for hit in hits)
    count = len(colours)
    order = (bad * (4 * levels) + cost) * count + jnp.arange(count, dtype=jnp.int32)
    chosen = jnp.arange(count, dtype=jnp.int32) == jnp.min(order) % count
    numbers = np.arange(len(perms), dtype=np.int32)
    picks = [
        jnp.sum(jnp.where(chosen[:, None] & hit, numbers[None, :], 0)) for hit in hits
    ]
    source = jnp.sum(jnp.where(chosen[:, None], colours, 0), axis=0)
    landing = jnp.sum(jnp.where(chosen[:, None], landed, 0), axis=0)
    return source, landing, picks, perms


def body(
    tokens, routes, gates, plan, proj_weight, proj_grad, first_moment, second_moment, down_weight
):
    owners = lax.axis_size("expert")
    local_rows = proj_weight.shape[2]
    width = proj_weight.shape[3]
    levels = owners // 2
    routable = levels <= max_levels and foldable(local_rows, width)

    def updated_rows(grads, a, b):
        return adam_update(
            proj_weight[0, :, a:b], grads[0, :, a:b], first_moment[0, :, a:b], second_moment[0, :, a:b]
        )

    group_tokens = tokens.shape[1]
    route_count = routes.shape[2]
    capacity = min(group_tokens, 3 * group_tokens * route_count // (2 * owners))
    down_local = down_weight[0]
    expert_ids = jnp.arange(owners, dtype=jnp.int32)
    target_match = routes[0][:, :, None] == expert_ids[None, None, :]
    routed = jnp.sum(target_match.astype(jnp.int32), axis=1)
    weighting = jnp.sum(jnp.where(target_match, gates[0][:, :, None], 0.0), axis=1)
    ranks = jnp.cumsum(routed, axis=0) - routed
    slot_ids = jnp.arange(capacity, dtype=jnp.int32)
    select = jnp.logical_and(
        ranks.T[:, None, :] == slot_ids[None, :, None], routed.T[:, None, :] > 0
    )
    dispatch_buf = jnp.einsum(
        "ost,td->osd", select.astype(jnp.bfloat16), tokens[0], preferred_element_type=jnp.float32
    ).astype(jnp.bfloat16)
    arrived = owner_exchange(dispatch_buf[None])
    slots = arrived.reshape(owners * capacity, local_rows)


    def experts(pieces):
        expert_out = finish_rows(dp_blocks(partial_products(slots, pieces)), down_local)
        return expert_out.reshape(1, owners, capacity, local_rows)

    if routable:
        early = early_rows(local_rows, width)
        new_proj, new_down, returned = routed_migration(
            plan,
            levels,
            updated_rows(proj_grad, 0, early),
            lambda grads: updated_rows(grads, early, local_rows),
            proj_grad,
            down_local,
            arrived,
            experts,
        )
    else:
        updated = updated_rows(proj_grad, 0, local_rows)
        new_proj, new_down = two_phase_migration(plan, updated, down_local)
        returned = owner_exchange(experts([updated]))
    combine = select.astype(jnp.float32) * weighting.T[:, None, :]
    mixed = jnp.einsum(
        "ost,osd->td", combine, returned[0].astype(jnp.float32), precision=lax.Precision.HIGHEST
    )
    return (mixed.astype(jnp.bfloat16)[None], new_proj[None], new_down[None])


def foldable(local_rows, width):
    extra = local_rows - width
    return extra > 0 and width % extra == 0 and (width // 2) % (width // extra) == 0


def early_rows(local_rows, width):
    return (local_rows - (width // 2) * local_rows // width) // 2


def fold(half, width):
    strips = width // (half.shape[1] - width)
    tall = half.shape[0] // strips
    rest = [half[i * tall : (i + 1) * tall, width:] for i in range(strips)]
    return [half[:, :width], jnp.concatenate(rest, axis=1)]


def unfold(packed, rows, columns):
    width = packed.shape[1]
    extra = columns - width
    strips = [packed[rows:, i * extra : (i + 1) * extra] for i in range(width // extra)]
    return jnp.concatenate([packed[:rows], jnp.concatenate(strips, axis=0)], axis=1)


def routed_migration(
    plan, levels, updated_early, late_rows, grads, down_local, arrived, experts
):
    source, landing, picks, perms = route_choice(plan, levels)
    me = lax.axis_index("expert")
    line = me % 2
    at_me = jnp.arange(2 * levels, dtype=jnp.int32) == me
    colour = jnp.sum(jnp.where(at_me, source, 0))
    landing_colour = jnp.sum(jnp.where(at_me, landing, 0))
    kept_half = line ^ colour
    final_half = line ^ landing_colour
    across = [(e, e ^ 1) for e in range(2 * levels)]
    local_rows, width = down_local.shape[1], updated_early.shape[2]
    half_width = width // 2
    folded = half_width * local_rows // width

    def swap(value):
        return lax.ppermute(value, "expert", across)

    def parted(first, second):
        keep = jnp.where(kept_half == 0, first, second)
        send = jnp.where(kept_half == 0, second, first)
        return keep, send

    def coloured(keep, other):
        first = jnp.where(colour == 0, keep, other)
        second = jnp.where(colour == 0, other, keep)
        return first, second

    packed = [
        jnp.concatenate(
            fold(down_local[h * half_width : (h + 1) * half_width], width)
            + [updated_early[h]],
            axis=0,
        )
        for h in (0, 1)
    ]
    keep_p, send_p = parted(*packed)
    send_p, grads, ahead = lax.optimization_barrier((send_p, grads, arrived))
    crossed_p = swap(send_p)
    updated_late = late_rows(grads)
    keep_q, send_q = parted(updated_late[0], updated_late[1])
    expert_out = experts([updated_early, updated_late])
    keep_p, crossed_p, keep_q, send_q, expert_out = lax.optimization_barrier(
        (keep_p, crossed_p, keep_q, send_q, expert_out)
    )

    def along(perm):
        pairs = [(2 * z + x, 2 * to + x) for z, to in enumerate(perm) for x in (0, 1)]
        return lambda value: lax.ppermute(value, "expert", pairs)

    def first_stage(perm):
        move = along(perm)
        return lambda value, crossing: (move(value), swap(crossing))

    def step(number, carry):
        keep, crossed, moved, arrived, unused = carry
        first, second = coloured(keep, crossed)
        own = jnp.where(landing_colour == 0, moved, arrived)
        other = jnp.where(landing_colour == 0, arrived, moved)
        crossing = jnp.where(number == 0, moved, other)
        moved, crossed = lax.switch(
            picks[0], [first_stage(p) for p in perms], first, crossing
        )
        arrived = lax.switch(picks[1], [along(p) for p in perms], second)
        return keep_q, crossed, moved, arrived, own

    unused, other_p, moved, arrived, own_p = lax.fori_loop(
        0, 2, step, (keep_p, crossed_p, send_q, send_q, send_q)
    )
    moved, arrived, expert_out = lax.optimization_barrier((moved, arrived, expert_out))
    returned = owner_exchange(expert_out)
    own_q = jnp.where(landing_colour == 0, moved, arrived)
    send_q = jnp.where(landing_colour == 0, arrived, moved)
    send_q, returned = lax.optimization_barrier((send_q, returned))
    other_q = swap(send_q)
    halves_p = [jnp.where(final_half == h, own_p, other_p) for h in (0, 1)]
    halves_q = [jnp.where(final_half == h, own_q, other_q) for h in (0, 1)]
    new_down = jnp.concatenate(
        [unfold(half[:folded], half_width, local_rows) for half in halves_p], axis=0
    )
    new_proj = jnp.stack(
        [jnp.concatenate([p[folded:], q], axis=0) for p, q in zip(halves_p, halves_q)]
    )
    return new_proj, new_down, returned


def solution(mesh):
    in_specs = (
        P("expert", None, "dp"),
        P("expert", None, None),
        P("expert", None, None),
        P(),
        P("expert", None, "dp", None),
        P("expert", None, "dp", None),
        P("expert", None, "dp", None),
        P("expert", None, "dp", None),
        P("expert", None, "dp"),
    )
    out_specs = (P("expert", None, "dp"), P("expert", None, "dp", None), P("expert", None, "dp"))
    return jax.shard_map(body, mesh=mesh, in_specs=in_specs, out_specs=out_specs, check_vma=False)
```

profile of v0, /device:TPU:0, one launch (start us, length us, event | category | flops | bytes accessed | tf_op | source)
XLA Modules:
  0.0 235.4 jit_solution(3542883411155437117)
XLA Ops:
  0.6 0.7 convert_reduce_fusion.1
  1.6 1.0 fusion.29
  2.6 7.3 %all-to-all-start = ((bf16[1,8,16,1024]{3,2,0,1:T(8,128)(2,1)}), bf16[1,8,16,1024]{3,2,0,1:T(8,128)(2,1)}, u32[]{:S(2)}, u32[]{:S(2)}) async-start(bf16[1,8,16,1024]{3,2,0,1:T(8,128)(2,1)} %fusion.29), calls=%async_computation | async-start | bytes 524288 | tf_op jit(solution)/shard_map/all_to_all | solution.py:64
  9.8 0.7 iota_compare_fusion.2
  10.6 0.7 fusion.57
  11.3 0.8 select_reduce_fusion
  12.1 0.8 select_reduce_fusion.4
  12.9 0.9 fusion.52
  13.7 0.6 add_reduce_fusion
  16.3 1.5 slice_bitcast_fusion.3
  18.1 0.5 copy-done.7
  18.6 0.1 select_reduce_fusion.3
  18.7 0.7 fusion.54
  19.5 0.6 fusion.56
  21.4 3.6 %fusion.25 = bf16[2,256,768]{2,1,0:T(8,128)(2,1)S(1)} fusion(f32[1,2,1024,768]{3,2,1,0:T(8,128)} %param.77, f32[1,2,1024,768]{3,2,1,0:T(8,128)} %param.76, bf16[1,2,1024,768]{3,2,1,0:T(8,128)(2,1)} %param.75, bf16[1,2,1024,768]{3,2,1,0:T(8,128)(2,1)} %param.74), kind=kLoop, calls=%fused_computation.63 | loop fusion | flops 6291456 | bytes 5505024 | tf_op jit(solution)/shard_map/convert_element_type | solution.py:22
  26.3 0.7 fusion.55
  27.6 3.7 %broadcast_select_fusion.32 = bf16[768,768]{1,0:T(8,128)(2,1)} fusion(pred[]{:T(512)S(6)} %eq.162, bf16[256,768]{1,0:T(8,128)(2,1)S(1)} %get-tuple-element.789, bf16[128,256]{1,0:T(8,128)(2,1)S(1)} %get-tuple-element.794, bf16[128,256]{1,0:T(8,128)(2,1)S(1)} %get-tuple-element.793, bf16[128,256]{1,0:T(8,128)(2,1)S(1)} %get-tuple-element.795, ...), kind=kLoop, calls=%fused_computation.76 | loop fusion | flops 12386304 | bytes 3538945 | tf_op jit(solution)/shard_map/jit(_where)/select_n | solution.py:229
  31.3 2.8 %broadcast_select_fusion.33 = bf16[768,768]{1,0:T(8,128)(2,1)S(1)} fusion(pred[]{:T(512)S(6)} %eq.162, bf16[256,768]{1,0:T(8,128)(2,1)S(1)} %get-tuple-element.789, bf16[128,256]{1,0:T(8,128)(2,1)S(1)} %get-tuple-element.794, bf16[128,256]{1,0:T(8,128)(2,1)S(1)} %get-tuple-element.793, bf16[128,256]{1,0:T(8,128)(2,1)S(1)} %get-tuple-element.795, ...), kind=kLoop, calls=%fused_computation.77 | loop fusion | flops 12386304 | bytes 3538945 | tf_op jit(solution)/shard_map/jit(_where)/select_n | solution.py:228
  34.1 7.0 %fusion.9 = bf16[2,768,768]{2,1,0:T(8,128)(2,1)S(1)} fusion(f32[1,2,1024,768]{3,2,1,0:T(8,128)} %param.77, f32[1,2,1024,768]{3,2,1,0:T(8,128)} %param.76, bf16[1,2,1024,768]{3,2,1,0:T(8,128)(2,1)} %param.75, bf16[1,2,1024,768]{3,2,1,0:T(8,128)(2,1)} %param.74), kind=kLoop, calls=%fused_computation.39 | loop fusion | flops 18874368 | bytes 16515072 | tf_op jit(solution)/shard_map/convert_element_type | solution.py:22
  41.1 0.2 slice_bitcast_fusion.1
  41.3 1.2 fusion.32
  42.5 2.1 collective-permute-start.72
  44.6 2.2 fusion.10
  46.8 4.1 %all-to-all-start.1 = ((bf16[1,4,32,1536]{3,2,0,1:T(8,128)(2,1)}), bf16[1,4,32,1536]{3,2,0,1:T(8,128)(2,1)}, u32[]{:S(2)}, u32[]{:S(2)}) async-start(bf16[1,4,32,1536]{3,2,0,1:T(8,128)(2,1)} %bitcast.28), calls=%async_computation.1 | async-start | bytes 786432 | tf_op jit(solution)/shard_map/all_to_all | solution.py:42
  50.9 2.9 %broadcast_select_fusion.30 = (bf16[768,768]{1,0:T(8,128)(2,1)}, bf16[768,768]{1,0:T(8,128)(2,1)S(1)}) fusion(pred[]{:T(512)S(6)} %eq.162, bf16[2,768,768]{2,1,0:T(8,128)(2,1)} %copy-done.2), kind=kLoop, calls=%fused_computation.74 | loop fusion | flops 1179648 | bytes 4718593 | tf_op jit(solution)/shard_map/jit(_where)/select_n | solution.py:229
  53.8 4.7 %all-to-all-done.1 = bf16[1,4,32,1536]{3,2,0,1:T(8,128)(2,1)} async-done(((bf16[1,4,32,1536]{3,2,0,1:T(8,128)(2,1)}), bf16[1,4,32,1536]{3,2,0,1:T(8,128)(2,1)}, u32[]{:S(2)}, u32[]{:S(2)}) %all-to-all-start.1) | async-done | bytes 393248 | tf_op jit(solution)/shard_map/all_to_all | solution.py:42
  58.4 1.1 convert_reduce_fusion
  59.5 5.8 %all_gather.3 = bf16[128,768]{1,0:T(8,128)(2,1)S(1)} all-gather(bf16[32,768]{1,0:T(8,128)(2,1)S(1)} %fusion.38), channel_id=1, replica_groups=mesh['dp'=4,'expert'=8] {'dp'}, dimensions={0}, use_global_device_ids=true | all-gather | bytes 245760 | tf_op jit(solution)/shard_map/all_gather | solution.py:56
  65.3 2.5 %fusion.26 = bf16[128,1024]{1,0:T(8,128)(2,1)} fusion(bf16[128,768]{1,0:T(8,128)(2,1)S(1)} %all_gather.3, bf16[1,768,1024]{2,1,0:T(8,128)(2,1)} %param.78), kind=kOutput, calls=%fused_computation.65 | convolution fusion | flops 201457664 | bytes 2031616 | tf_op jit(solution)/shard_map/dot_general | solution.py:55
  67.8 2.4 %collective-permute-done.72 = bf16[768,768]{1,0:T(8,128)(2,1)S(1)} collective-permute-done((bf16[768,768]{1,0:T(8,128)(2,1)}, bf16[768,768]{1,0:T(8,128)(2,1)S(1)}, u32[]{:S(2)}, u32[]{:S(2)}) %collective-permute-start.72) | collective-permute-done | bytes 1179680 | tf_op jit(solution)/shard_map/ppermute | solution.py:225
  70.2 2.4 %copy.122 = bf16[768,768]{1,0:T(8,128)(2,1)} copy(bf16[768,768]{1,0:T(8,128)(2,1)} %get-tuple-element.924) | data formatting | bytes 2359296
  72.6 2.4 %copy.123 = bf16[768,768]{1,0:T(8,128)(2,1)} copy(bf16[768,768]{1,0:T(8,128)(2,1)} %get-tuple-element.924) | data formatting | bytes 2359296
  75.0 122.0 %while.23 = (s32[]{:T(128)}, bf16[768,768]{1,0:T(8,128)(2,1)S(1)}, bf16[768,768]{1,0:T(8,128)(2,1)S(1)}, bf16[768,768]{1,0:T(8,128)(2,1)}, bf16[768,768]{1,0:T(8...) while((s32[]{:T(128)}, bf16[768,768]{1,0:T(8,128)(2,1)S(1)}, ...), condition=%wide.region_67.68_spmd, body=%wide.region_18.67_spmd.sunk | while | flops 2949123 | bytes 30671168 | solution.py:275
  75.0 2.9 %broadcast_select_fusion.37 = (bf16[768,768]{1,0:T(8,128)(2,1)}, bf16[768,768]{1,0:T(8,128)(2,1)S(1)}, bf16[768,768]{1,0:T(8,128)(2,1)S(1)}) fusion(bf16[768,768]{1,0:T(8,128)(2,1)} %get-tuple-element.935, bf16[768,768]{1,0:T(8,128)(2,1)} %get-tuple-element.936, pred[]{:T(512)} %get-tuple-element.952, pred[]{:T(512)S(6)} %eq.234, ...), kind=kLoop, calls=%fused_computation.25.clone.1 | loop fusion | flops 2359296 | bytes 8257539 | tf_op jit(solution)/shard_map/while/body/eval_jaxpr/jit(_where)/select_n | solution.py:266
  77.9 29.8 %conditional.4 = (bf16[768,768]{1,0:T(8,128)(2,1)}, bf16[768,768]{1,0:T(8,128)(2,1)}) conditional(s32[]{:T(128)} %get-tuple-element.953, (bf16[768,768]{1,0:T(8,128)(2,1)S(1)}, bf16[768,768]{1,0:T(8,128)(2,1)S(1)}) %tuple.272, (bf16[768,768]{1,0:T(8,128)(2,1)S(1)}, bf16[768,768]{1,0:T(8,128)(2,1)S(1)}) %tuple.272, ...), branch_computations={%region_19.19_spmd, %region_20.20_spmd, %region_21.21_spmd, %regio... | conditional | bytes 9437280 | solution.py:269
  77.9 3.6 %collective-permute-start.16 = (bf16[768,768]{1,0:T(8,128)(2,1)S(1)}, bf16[768,768]{1,0:T(8,128)(2,1)}, u32[]{:S(2)}, u32[]{:S(2)}) collective-permute-start(bf16[768,768]{1,0:T(8,128)(2,1)S(1)} %get-tuple-element.584), channel_id=1, source_target_pairs={{0,2},{1,3},{2,4},{3,5},{4,0},{5,1},{6,6},{7,7},{8,10},{9,11},{10,... | collective-permute-start | bytes 3538952 | tf_op jit(solution)/shard_map/while/body/eval_jaxpr/cond/branch_8_fun/ppermute | solution.py:257
  81.5 1.5 collective-permute-start.17
  83.1 24.2 %collective-permute-done.16 = bf16[768,768]{1,0:T(8,128)(2,1)} collective-permute-done((bf16[768,768]{1,0:T(8,128)(2,1)S(1)}, bf16[768,768]{1,0:T(8,128)(2,1)}, u32[]{:S(2)}, u32[]{:S(2)}) %collective-permute-start.16) | collective-permute-done | bytes 1179680 | tf_op jit(solution)/shard_map/while/body/eval_jaxpr/cond/branch_8_fun/ppermute | solution.py:257
  107.3 0.4 collective-permute-done.17
  107.7 29.2 %conditional.5 = (bf16[768,768]{1,0:T(8,128)(2,1)}) conditional(s32[]{:T(128)} %get-tuple-element.954, (pred[]{:T(512)}, bf16[768,768]{1,0:T(8,128)(2,1)S(1)}, bf16[768,768]{1,0:T(8,128)(2,1)S(1)}) %tuple.273, (pred[]{:T(512)}, bf16[768,768]{1,0:T(8,128)(2,1)S(1)}, bf16[768,768]{1,0:T(8,128)(2,1)S(1)}) %tuple.273, ...), branch_computations={%region_43.43_spmd, %region_44.44_spmd, %region_45.45_spmd, %regio... | conditional | flops 589824 | bytes 8257585 | solution.py:272
  107.7 0.1 broadcast_select_fusion.21
  107.8 3.7 %collective-permute-start.69 = (bf16[768,768]{1,0:T(8,128)(2,1)S(1)}, bf16[768,768]{1,0:T(8,128)(2,1)}, u32[]{:S(2)}, u32[]{:S(2)}) collective-permute-start(bf16[768,768]{1,0:T(8,128)(2,1)S(1)} %broadcast_select_fusion.21), channel_id=1, source_target_pairs={{0,6},{1,7},{2,2},{3,3},{4,4},{5,5},{6,0},{7,1},{8,14},{9,15},{10,... | collective-permute-start | bytes 3538952 | tf_op jit(solution)/shard_map/while/body/eval_jaxpr/cond/branch_21_fun/ppermute | solution.py:257
  111.5 25.3 %collective-permute-done.69 = bf16[768,768]{1,0:T(8,128)(2,1)} collective-permute-done((bf16[768,768]{1,0:T(8,128)(2,1)S(1)}, bf16[768,768]{1,0:T(8,128)(2,1)}, u32[]{:S(2)}, u32[]{:S(2)}) %collective-permute-start.69) | collective-permute-done | bytes 1179680 | tf_op jit(solution)/shard_map/while/body/eval_jaxpr/cond/branch_21_fun/ppermute | solution.py:257
  136.8 1.3 copy.132
  138.2 2.9 %broadcast_select_fusion.37 = (bf16[768,768]{1,0:T(8,128)(2,1)}, bf16[768,768]{1,0:T(8,128)(2,1)S(1)}, bf16[768,768]{1,0:T(8,128)(2,1)S(1)}) fusion(bf16[768,768]{1,0:T(8,128)(2,1)} %get-tuple-element.935, bf16[768,768]{1,0:T(8,128)(2,1)} %get-tuple-element.936, pred[]{:T(512)} %get-tuple-element.952, pred[]{:T(512)S(6)} %eq.234, ...), kind=kLoop, calls=%fused_computation.25.clone.1 | loop fusion | flops 2359296 | bytes 8257539 | tf_op jit(solution)/shard_map/while/body/eval_jaxpr/jit(_where)/select_n | solution.py:266
  141.1 27.2 %conditional.4 = (bf16[768,768]{1,0:T(8,128)(2,1)}, bf16[768,768]{1,0:T(8,128)(2,1)}) conditional(s32[]{:T(128)} %get-tuple-element.953, (bf16[768,768]{1,0:T(8,128)(2,1)S(1)}, bf16[768,768]{1,0:T(8,128)(2,1)S(1)}) %tuple.272, (bf16[768,768]{1,0:T(8,128)(2,1)S(1)}, bf16[768,768]{1,0:T(8,128)(2,1)S(1)}) %tuple.272, ...), branch_computations={%region_19.19_spmd, %region_20.20_spmd, %region_21.21_spmd, %regio... | conditional | bytes 9437280 | solution.py:269
  141.1 1.9 collective-permute-start.16
  143.0 1.3 collective-permute-start.17
  144.3 24.0 %collective-permute-done.16 = bf16[768,768]{1,0:T(8,128)(2,1)} collective-permute-done((bf16[768,768]{1,0:T(8,128)(2,1)S(1)}, bf16[768,768]{1,0:T(8,128)(2,1)}, u32[]{:S(2)}, u32[]{:S(2)}) %collective-permute-start.16) | collective-permute-done | bytes 1179680 | tf_op jit(solution)/shard_map/while/body/eval_jaxpr/cond/branch_8_fun/ppermute | solution.py:257
  168.3 27.3 %conditional.5 = (bf16[768,768]{1,0:T(8,128)(2,1)}) conditional(s32[]{:T(128)} %get-tuple-element.954, (pred[]{:T(512)}, bf16[768,768]{1,0:T(8,128)(2,1)S(1)}, bf16[768,768]{1,0:T(8,128)(2,1)S(1)}) %tuple.273, (pred[]{:T(512)}, bf16[768,768]{1,0:T(8,128)(2,1)S(1)}, bf16[768,768]{1,0:T(8,128)(2,1)S(1)}) %tuple.273, ...), branch_computations={%region_43.43_spmd, %region_44.44_spmd, %region_45.45_spmd, %regio... | conditional | flops 589824 | bytes 8257585 | solution.py:272
  168.3 0.1 broadcast_select_fusion.21
  168.4 2.8 %collective-permute-start.69 = (bf16[768,768]{1,0:T(8,128)(2,1)S(1)}, bf16[768,768]{1,0:T(8,128)(2,1)}, u32[]{:S(2)}, u32[]{:S(2)}) collective-permute-start(bf16[768,768]{1,0:T(8,128)(2,1)S(1)} %broadcast_select_fusion.21), channel_id=1, source_target_pairs={{0,6},{1,7},{2,2},{3,3},{4,4},{5,5},{6,0},{7,1},{8,14},{9,15},{10,... | collective-permute-start | bytes 3538952 | tf_op jit(solution)/shard_map/while/body/eval_jaxpr/cond/branch_21_fun/ppermute | solution.py:257
  171.3 24.4 %collective-permute-done.69 = bf16[768,768]{1,0:T(8,128)(2,1)} collective-permute-done((bf16[768,768]{1,0:T(8,128)(2,1)S(1)}, bf16[768,768]{1,0:T(8,128)(2,1)}, u32[]{:S(2)}, u32[]{:S(2)}) %collective-permute-start.69) | collective-permute-done | bytes 1179680 | tf_op jit(solution)/shard_map/while/body/eval_jaxpr/cond/branch_21_fun/ppermute | solution.py:257
  195.6 1.3 copy.132
  197.0 4.3 %all-to-all-start.2 = ((bf16[1,8,16,1024]{3,2,0,1:T(8,128)(2,1)}), bf16[1,8,16,1024]{3,2,0,1:T(8,128)(2,1)}, u32[]{:S(2)}, u32[]{:S(2)}) async-start(bf16[1,8,16,1024]{3,2,0,1:T(8,128)(2,1)} %bitcast.95), calls=%async_computation.2 | async-start | bytes 524288 | tf_op jit(solution)/shard_map/all_to_all | solution.py:64
  202.0 1.5 broadcast_select_fusion.35
  203.5 5.9 %all-to-all-done.2 = bf16[1,8,16,1024]{3,2,0,1:T(8,128)(2,1)} async-done(((bf16[1,8,16,1024]{3,2,0,1:T(8,128)(2,1)}), bf16[1,8,16,1024]{3,2,0,1:T(8,128)(2,1)}, u32[]{:S(2)}, u32[]{:S(2)}) %all-to-all-start.2) | async-done | bytes 262176 | tf_op jit(solution)/shard_map/all_to_all | solution.py:64
  209.4 0.2 broadcast_select_fusion.29
  209.8 5.4 %maximum_bitcast_fusion.3 = bf16[1,768,1024]{2,1,0:T(8,128)(2,1)} fusion(bf16[128,256]{1,0:T(8,128)(2,1)S(1)} %get-tuple-element.783, bf16[128,256]{1,0:T(8,128)(2,1)S(1)} %get-tuple-element.784, bf16[128,256]{1,0:T(8,128)(2,1)S(1)} %get-tuple-element.782, bf16[384,768]{1,0:T(8,128)(2,1)S(1)} %slice.188, bf16[128,256]{1,0:T(8,128)(2,1)S(1)} %get-tuple-element.780, ...), kind=kLoop, calls=%fused_computation.60 | loop fusion | flops 12582912 | bytes 3145728 | tf_op jit(solution)/shard_map/broadcast_in_dim | solution.py:182
  215.2 2.1 fusion.31
  217.3 14.4 %collective-permute-done.73 = bf16[768,768]{1,0:T(8,128)(2,1)S(1)} collective-permute-done((bf16[768,768]{1,0:T(8,128)(2,1)S(1)}, bf16[768,768]{1,0:T(8,128)(2,1)S(1)}, u32[]{:S(2)}, u32[]{:S(2)}) %collective-permute-start.73) | collective-permute-done | bytes 1179680 | tf_op jit(solution)/shard_map/ppermute | solution.py:225
  231.7 1.6 broadcast_select_fusion.28
  233.2 0.1 maximum_bitcast_fusion.1
  233.5 1.9 maximum_bitcast_fusion
  (49 shorter events, 1.0 us)
Async XLA Ops:
  0.6 0.9 copy-start
  1.4 16.4 %copy-start.8 = (pred[8,16]{1,0:T(8,128)(4,1)}, pred[8,16]{1,0:T(8,128)(4,1)S(1)}, u32[]{:S(2)}) copy-start(pred[8,16]{1,0:T(8,128)(4,1)S(1)} %compare_bitcast_fusion) | copy-start | bytes 388
  1.6 16.3 %copy-start.4 = (s32[8,16]{1,0:T(8,128)}, s32[8,16]{1,0:T(8,128)S(1)}, u32[]{:S(2)}) copy-start(s32[8,16]{1,0:T(8,128)S(1)} %copy.40) | copy-start | bytes 1540
  2.6 31.5 %all-to-all-start = ((bf16[1,8,16,1024]{3,2,0,1:T(8,128)(2,1)}), bf16[1,8,16,1024]{3,2,0,1:T(8,128)(2,1)}, u32[]{:S(2)}, u32[]{:S(2)}) async-start(bf16[1,8,16,1024]{3,2,0,1:T(8,128)(2,1)} %fusion.29), calls=%async_computation | async-start | bytes 524288 | tf_op jit(solution)/shard_map/all_to_all | solution.py:64
  17.9 0.7 copy-start.7
  17.9 0.8 copy-start.11
  41.1 5.7 %copy-start.2 = (bf16[2,768,768]{2,1,0:T(8,128)(2,1)}, bf16[2,768,768]{2,1,0:T(8,128)(2,1)S(1)}, u32[]{:S(2)}) copy-start(bf16[2,768,768]{2,1,0:T(8,128)(2,1)S(1)} %fusion.9) | copy-start | bytes 7077892
  42.5 27.7 %collective-permute-start.72 = (bf16[768,768]{1,0:T(8,128)(2,1)}, bf16[768,768]{1,0:T(8,128)(2,1)S(1)}, u32[]{:S(2)}, u32[]{:S(2)}) collective-permute-start(bf16[768,768]{1,0:T(8,128)(2,1)} %broadcast_select_fusion.32), channel_id=1, source_target_pairs={{0,1},{1,0},{2,3},{3,2},{4,5},{5,4},{6,7},{7,6},{8,9},{9,8},{10,11... | collective-permute-start | bytes 3538952 | tf_op jit(solution)/shard_map/ppermute | solution.py:225
  46.8 11.6 %all-to-all-start.1 = ((bf16[1,4,32,1536]{3,2,0,1:T(8,128)(2,1)}), bf16[1,4,32,1536]{3,2,0,1:T(8,128)(2,1)}, u32[]{:S(2)}, u32[]{:S(2)}) async-start(bf16[1,4,32,1536]{3,2,0,1:T(8,128)(2,1)} %bitcast.28), calls=%async_computation.1 | async-start | bytes 786432 | tf_op jit(solution)/shard_map/all_to_all | solution.py:42
  75.0 127.0 %copy-start.6 = (s32[1,16,8]{1,2,0:T(8,128)S(1)}, s32[1,16,8]{1,2,0:T(8,128)}, u32[]{:S(2)}) copy-start(s32[1,16,8]{1,2,0:T(8,128)} %param.71) | copy-start | bytes 1540
  75.0 127.0 %copy-start.10 = (f32[1,16,8]{1,2,0:T(8,128)S(1)}, f32[1,16,8]{1,2,0:T(8,128)}, u32[]{:S(2)}) copy-start(f32[1,16,8]{1,2,0:T(8,128)} %param.72) | copy-start | bytes 1540
  77.9 29.4 %collective-permute-start.16 = (bf16[768,768]{1,0:T(8,128)(2,1)S(1)}, bf16[768,768]{1,0:T(8,128)(2,1)}, u32[]{:S(2)}, u32[]{:S(2)}) collective-permute-start(bf16[768,768]{1,0:T(8,128)(2,1)S(1)} %get-tuple-element.584), channel_id=1, source_target_pairs={{0,2},{1,3},{2,4},{3,5},{4,0},{5,1},{6,6},{7,7},{8,10},{9,11},{10,... | collective-permute-start | bytes 3538952 | tf_op jit(solution)/shard_map/while/body/eval_jaxpr/cond/branch_8_fun/ppermute | solution.py:257
  81.5 26.1 %collective-permute-start.17 = (bf16[768,768]{1,0:T(8,128)(2,1)S(1)}, bf16[768,768]{1,0:T(8,128)(2,1)}, u32[]{:S(2)}, u32[]{:S(2)}) collective-permute-start(bf16[768,768]{1,0:T(8,128)(2,1)S(1)} %get-tuple-element.585), channel_id=1, source_target_pairs={{0,1},{1,0},{2,3},{3,2},{4,5},{5,4},{6,7},{7,6},{8,9},{9,8},{10,11... | collective-permute-start | bytes 3538952 | tf_op jit(solution)/shard_map/while/body/eval_jaxpr/cond/branch_8_fun/ppermute | solution.py:225
  107.8 29.0 %collective-permute-start.69 = (bf16[768,768]{1,0:T(8,128)(2,1)S(1)}, bf16[768,768]{1,0:T(8,128)(2,1)}, u32[]{:S(2)}, u32[]{:S(2)}) collective-permute-start(bf16[768,768]{1,0:T(8,128)(2,1)S(1)} %broadcast_select_fusion.21), channel_id=1, source_target_pairs={{0,6},{1,7},{2,2},{3,3},{4,4},{5,5},{6,0},{7,1},{8,14},{9,15},{10,... | collective-permute-start | bytes 3538952 | tf_op jit(solution)/shard_map/while/body/eval_jaxpr/cond/branch_21_fun/ppermute | solution.py:257
  141.1 27.2 %collective-permute-start.16 = (bf16[768,768]{1,0:T(8,128)(2,1)S(1)}, bf16[768,768]{1,0:T(8,128)(2,1)}, u32[]{:S(2)}, u32[]{:S(2)}) collective-permute-start(bf16[768,768]{1,0:T(8,128)(2,1)S(1)} %get-tuple-element.584), channel_id=1, source_target_pairs={{0,2},{1,3},{2,4},{3,5},{4,0},{5,1},{6,6},{7,7},{8,10},{9,11},{10,... | collective-permute-start | bytes 3538952 | tf_op jit(solution)/shard_map/while/body/eval_jaxpr/cond/branch_8_fun/ppermute | solution.py:257
  143.0 25.3 %collective-permute-start.17 = (bf16[768,768]{1,0:T(8,128)(2,1)S(1)}, bf16[768,768]{1,0:T(8,128)(2,1)}, u32[]{:S(2)}, u32[]{:S(2)}) collective-permute-start(bf16[768,768]{1,0:T(8,128)(2,1)S(1)} %get-tuple-element.585), channel_id=1, source_target_pairs={{0,1},{1,0},{2,3},{3,2},{4,5},{5,4},{6,7},{7,6},{8,9},{9,8},{10,11... | collective-permute-start | bytes 3538952 | tf_op jit(solution)/shard_map/while/body/eval_jaxpr/cond/branch_8_fun/ppermute | solution.py:225
  168.4 27.2 %collective-permute-start.69 = (bf16[768,768]{1,0:T(8,128)(2,1)S(1)}, bf16[768,768]{1,0:T(8,128)(2,1)}, u32[]{:S(2)}, u32[]{:S(2)}) collective-permute-start(bf16[768,768]{1,0:T(8,128)(2,1)S(1)} %broadcast_select_fusion.21), channel_id=1, source_target_pairs={{0,6},{1,7},{2,2},{3,3},{4,4},{5,5},{6,0},{7,1},{8,14},{9,15},{10,... | collective-permute-start | bytes 3538952 | tf_op jit(solution)/shard_map/while/body/eval_jaxpr/cond/branch_21_fun/ppermute | solution.py:257
  197.0 12.4 %all-to-all-start.2 = ((bf16[1,8,16,1024]{3,2,0,1:T(8,128)(2,1)}), bf16[1,8,16,1024]{3,2,0,1:T(8,128)(2,1)}, u32[]{:S(2)}, u32[]{:S(2)}) async-start(bf16[1,8,16,1024]{3,2,0,1:T(8,128)(2,1)} %bitcast.95), calls=%async_computation.2 | async-start | bytes 524288 | tf_op jit(solution)/shard_map/all_to_all | solution.py:64
  202.0 7.5 %copy-start.3 = (bf16[768,768]{1,0:T(8,128)(2,1)S(1)}, bf16[768,768]{1,0:T(8,128)(2,1)}, u32[]{:S(2)}) copy-start(bf16[768,768]{1,0:T(8,128)(2,1)} %get-tuple-element.733) | copy-start | bytes 3538948
  209.4 22.3 %collective-permute-start.73 = (bf16[768,768]{1,0:T(8,128)(2,1)S(1)}, bf16[768,768]{1,0:T(8,128)(2,1)S(1)}, u32[]{:S(2)}, u32[]{:S(2)}) collective-permute-start(bf16[768,768]{1,0:T(8,128)(2,1)S(1)} %broadcast_select_fusion.35), channel_id=1, source_target_pairs={{0,1},{1,0},{2,3},{3,2},{4,5},{5,4},{6,7},{7,6},{8,9},{9,8},{10,11... | collective-permute-start | bytes 3538952 | tf_op jit(solution)/shard_map/ppermute | solution.py:225
  209.8 5.4 %copy-start.5 = (s32[8,16]{1,0:T(8,128)S(1)}, s32[8,16]{1,0:T(8,128)}, u32[]{:S(2)}) copy-start(s32[8,16]{1,0:T(8,128)} %copy-done.4) | copy-start | bytes 1540
  209.8 5.4 %copy-start.9 = (pred[8,16]{1,0:T(8,128)(4,1)S(1)}, pred[8,16]{1,0:T(8,128)(4,1)}, u32[]{:S(2)}) copy-start(pred[8,16]{1,0:T(8,128)(4,1)} %copy-done.8) | copy-start | bytes 388
  233.5 2.0 copy-start.1
where the time goes:
time: 236 us; the launch traced here: 235 us
  waiting for transfers between devices  126 us (53%)
  other arithmetic  45.3 us (19%)
  starting transfers between devices  32.7 us (14%)
  local copies, waits for them, and re-layouts  10.2 us (4%)
  matrix products  9.02 us (4%)
  between operations  6.77 us (3%)
  blocking collectives  5.79 us (2%)
    ppermute x4, waiting for transfers between devices, along(): return lambda value: lax.ppermute(value, 'expert', pairs)  97.9 us
    ppermute x4, waiting for transfers between devices, swap(): return lax.ppermute(value, 'expert', across)  17.1 us
    ppermute x4, starting transfers between devices, along(): return lambda value: lax.ppermute(value, 'expert', pairs)  12.1 us
    all_to_all x2, starting transfers between devices, owner_exchange(): lax.all_to_all(pieces, 'expert', split_axis=1, concat_axis=1, tiled=True)  11.5 us
    convert_element_type x2, other arithmetic, adam_update(): (weights.astype(jnp.float32) - learning_rate * adam_step).astype(jnp.bflo...  10.6 us
    broadcast_in_dim x2, other arithmetic, body(): return (mixed.astype(jnp.bfloat16)[None], new_proj[None], new_down[None])  7.33 us
    select_n x2, other arithmetic, parted(): send = jnp.where(kept_half == 0, second, first)  6.54 us
    all_to_all x2, waiting for transfers between devices, owner_exchange(): lax.all_to_all(pieces, 'expert', split_axis=1, concat_axis=1, tiled=True)  5.93 us
  transfers between devices with their start and end apart: 11, of which 9 were waited for; matrix products, arithmetic and copies ran while one was open for 15% of the time, Pallas kernels for 0%

commit v1 on v0

--- a/solution.py
+++ b/solution.py
@@ -272,8 +272,9 @@
         arrived = lax.switch(picks[1], [along(p) for p in perms], second)
         return keep_q, crossed, moved, arrived, own
 
+    blank = jnp.zeros_like(send_q)
     unused, other_p, moved, arrived, own_p = lax.fori_loop(
-        0, 2, step, (keep_p, crossed_p, send_q, send_q, send_q)
+        0, 2, step, (keep_p, crossed_p, send_q, blank, blank)
     )
     moved, arrived, expert_out = lax.optimization_barrier((moved, arrived, expert_out))
     returned = owner_exchange(expert_out)

time: 236 us -> 229 us (0.970)
  waiting for transfers between devices: 126 us -> 119 us
  starting transfers between devices: 32.7 us -> 37.8 us
  local copies, waits for them, and re-layouts: 10.2 us -> 6.58 us
    ppermute x4, waiting for transfers between devices: 97.9 us -> 44 us  [along(): return lambda value: lax.ppermute(value, 'expert', pairs)]
    ppermute x4, waiting for transfers between devices: 17.1 us -> 64.5 us  [swap(): return lax.ppermute(value, 'expert', across)]
    unnamed x26 -> x24, local copies, waits for them, and re-layouts: 5.32 us -> 0.58 us
    ppermute x4, starting transfers between devices: 12.1 us -> 14.5 us  [along(): return lambda value: lax.ppermute(value, 'expert', pairs)]
  transfers between devices with their start and end apart: 11 -> 11, of which waited for: 9 -> 8; matrix products, arithmetic and copies ran while one was open for 15% -> 16% of each run, Pallas kernels for 0% -> 0%
where the time goes in v1:
time: 229 us; the launch traced here: 231 us
  waiting for transfers between devices  119 us (52%)
  other arithmetic  45.3 us (20%)
  starting transfers between devices  37.8 us (17%)
  matrix products  9.02 us (4%)
  between operations  6.69 us (3%)
  local copies, waits for them, and re-layouts  6.58 us (3%)
  blocking collectives  5.79 us (3%)
    ppermute x4, waiting for transfers between devices, swap(): return lax.ppermute(value, 'expert', across)  64.5 us
    ppermute x4, waiting for transfers between devices, along(): return lambda value: lax.ppermute(value, 'expert', pairs)  44 us
    ppermute x4, starting transfers between devices, along(): return lambda value: lax.ppermute(value, 'expert', pairs)  14.5 us
    all_to_all x2, starting transfers between devices, owner_exchange(): lax.all_to_all(pieces, 'expert', split_axis=1, concat_axis=1, tiled=True)  13.8 us
    convert_element_type x2, other arithmetic, adam_update(): (weights.astype(jnp.float32) - learning_rate * adam_step).astype(jnp.bflo...  10.6 us
    broadcast_in_dim x2, other arithmetic, body(): return (mixed.astype(jnp.bfloat16)[None], new_proj[None], new_down[None])  7.33 us
    select_n x2, other arithmetic, parted(): send = jnp.where(kept_half == 0, second, first)  6.49 us
    all_to_all x2, waiting for transfers between devices, owner_exchange(): lax.all_to_all(pieces, 'expert', split_axis=1, concat_axis=1, tiled=True)  6.25 us
  transfers between devices with their start and end apart: 11, of which 8 were waited for; matrix products, arithmetic and copies ran while one was open for 16% of the time, Pallas kernels for 0%

profile of v1, /device:TPU:0, one launch (start us, length us, event | category | flops | bytes accessed | tf_op | source)
XLA Modules:
  0.0 230.7 jit_solution(17744376132747533197)
XLA Ops:
  0.6 0.7 convert_reduce_fusion.1
  1.6 1.0 fusion.29
  2.6 7.3 %all-to-all-start = ((bf16[1,8,16,1024]{3,2,0,1:T(8,128)(2,1)}), bf16[1,8,16,1024]{3,2,0,1:T(8,128)(2,1)}, u32[]{:S(2)}, u32[]{:S(2)}) async-start(bf16[1,8,16,1024]{3,2,0,1:T(8,128)(2,1)} %fusion.29), calls=%async_computation | async-start | bytes 524288 | tf_op jit(solution)/shard_map/all_to_all | solution.py:64
  9.8 0.7 iota_compare_fusion.2
  10.6 0.7 fusion.57
  11.3 0.8 select_reduce_fusion
  12.1 0.8 select_reduce_fusion.4
  12.9 0.9 fusion.52
  13.7 0.6 add_reduce_fusion
  16.3 1.5 slice_bitcast_fusion.3
  18.1 0.5 copy-done.7
  18.6 0.1 select_reduce_fusion.3
  18.7 0.7 fusion.54
  19.4 0.6 fusion.56
  21.4 3.6 %fusion.25 = bf16[2,256,768]{2,1,0:T(8,128)(2,1)S(1)} fusion(f32[1,2,1024,768]{3,2,1,0:T(8,128)} %param.77, f32[1,2,1024,768]{3,2,1,0:T(8,128)} %param.76, bf16[1,2,1024,768]{3,2,1,0:T(8,128)(2,1)} %param.75, bf16[1,2,1024,768]{3,2,1,0:T(8,128)(2,1)} %param.74), kind=kLoop, calls=%fused_computation.63 | loop fusion | flops 6291456 | bytes 5505024 | tf_op jit(solution)/shard_map/convert_element_type | solution.py:22
  26.2 0.6 fusion.55
  27.5 3.7 %broadcast_select_fusion.32 = bf16[768,768]{1,0:T(8,128)(2,1)} fusion(pred[]{:T(512)S(6)} %eq.162, bf16[256,768]{1,0:T(8,128)(2,1)S(1)} %get-tuple-element.789, bf16[128,256]{1,0:T(8,128)(2,1)S(1)} %get-tuple-element.794, bf16[128,256]{1,0:T(8,128)(2,1)S(1)} %get-tuple-element.793, bf16[128,256]{1,0:T(8,128)(2,1)S(1)} %get-tuple-element.795, ...), kind=kLoop, calls=%fused_computation.76 | loop fusion | flops 12386304 | bytes 3538945 | tf_op jit(solution)/shard_map/jit(_where)/select_n | solution.py:229
  31.2 2.8 %broadcast_select_fusion.33 = bf16[768,768]{1,0:T(8,128)(2,1)S(1)} fusion(pred[]{:T(512)S(6)} %eq.162, bf16[256,768]{1,0:T(8,128)(2,1)S(1)} %get-tuple-element.789, bf16[128,256]{1,0:T(8,128)(2,1)S(1)} %get-tuple-element.794, bf16[128,256]{1,0:T(8,128)(2,1)S(1)} %get-tuple-element.793, bf16[128,256]{1,0:T(8,128)(2,1)S(1)} %get-tuple-element.795, ...), kind=kLoop, calls=%fused_computation.77 | loop fusion | flops 12386304 | bytes 3538945 | tf_op jit(solution)/shard_map/jit(_where)/select_n | solution.py:228
  34.0 7.0 %fusion.9 = bf16[2,768,768]{2,1,0:T(8,128)(2,1)S(1)} fusion(f32[1,2,1024,768]{3,2,1,0:T(8,128)} %param.77, f32[1,2,1024,768]{3,2,1,0:T(8,128)} %param.76, bf16[1,2,1024,768]{3,2,1,0:T(8,128)(2,1)} %param.75, bf16[1,2,1024,768]{3,2,1,0:T(8,128)(2,1)} %param.74), kind=kLoop, calls=%fused_computation.39 | loop fusion | flops 18874368 | bytes 16515072 | tf_op jit(solution)/shard_map/convert_element_type | solution.py:22
  41.0 0.2 slice_bitcast_fusion.1
  41.2 1.2 fusion.32
  42.4 2.1 collective-permute-start.72
  44.5 2.2 fusion.10
  46.7 4.1 %all-to-all-start.1 = ((bf16[1,4,32,1536]{3,2,0,1:T(8,128)(2,1)}), bf16[1,4,32,1536]{3,2,0,1:T(8,128)(2,1)}, u32[]{:S(2)}, u32[]{:S(2)}) async-start(bf16[1,4,32,1536]{3,2,0,1:T(8,128)(2,1)} %bitcast.28), calls=%async_computation.1 | async-start | bytes 786432 | tf_op jit(solution)/shard_map/all_to_all | solution.py:42
  50.8 2.8 %broadcast_select_fusion.30 = (bf16[768,768]{1,0:T(8,128)(2,1)}, bf16[768,768]{1,0:T(8,128)(2,1)S(1)}) fusion(pred[]{:T(512)S(6)} %eq.162, bf16[2,768,768]{2,1,0:T(8,128)(2,1)} %copy-done.2), kind=kLoop, calls=%fused_computation.74 | loop fusion | flops 1179648 | bytes 4718593 | tf_op jit(solution)/shard_map/jit(_where)/select_n | solution.py:229
  53.6 4.7 %all-to-all-done.1 = bf16[1,4,32,1536]{3,2,0,1:T(8,128)(2,1)} async-done(((bf16[1,4,32,1536]{3,2,0,1:T(8,128)(2,1)}), bf16[1,4,32,1536]{3,2,0,1:T(8,128)(2,1)}, u32[]{:S(2)}, u32[]{:S(2)}) %all-to-all-start.1) | async-done | bytes 393248 | tf_op jit(solution)/shard_map/all_to_all | solution.py:42
  58.3 1.1 convert_reduce_fusion
  59.4 5.8 %all_gather.3 = bf16[128,768]{1,0:T(8,128)(2,1)S(1)} all-gather(bf16[32,768]{1,0:T(8,128)(2,1)S(1)} %fusion.38), channel_id=1, replica_groups=mesh['dp'=4,'expert'=8] {'dp'}, dimensions={0}, use_global_device_ids=true | all-gather | bytes 245760 | tf_op jit(solution)/shard_map/all_gather | solution.py:56
  65.2 2.5 %fusion.26 = bf16[128,1024]{1,0:T(8,128)(2,1)} fusion(bf16[128,768]{1,0:T(8,128)(2,1)S(1)} %all_gather.3, bf16[1,768,1024]{2,1,0:T(8,128)(2,1)} %param.78), kind=kOutput, calls=%fused_computation.65 | convolution fusion | flops 201457664 | bytes 2031616 | tf_op jit(solution)/shard_map/dot_general | solution.py:55
  67.7 2.4 %collective-permute-done.72 = bf16[768,768]{1,0:T(8,128)(2,1)S(1)} collective-permute-done((bf16[768,768]{1,0:T(8,128)(2,1)}, bf16[768,768]{1,0:T(8,128)(2,1)S(1)}, u32[]{:S(2)}, u32[]{:S(2)}) %collective-permute-start.72) | collective-permute-done | bytes 1179680 | tf_op jit(solution)/shard_map/ppermute | solution.py:225
  70.1 1.1 broadcast_in_dim.155
  71.3 118.6 %while.23 = (s32[]{:T(128)}, bf16[768,768]{1,0:T(8,128)(2,1)S(1)}, bf16[768,768]{1,0:T(8,128)(2,1)S(1)}, bf16[768,768]{1,0:T(8,128)(2,1)}, bf16[768,768]{1,0:T(8...) while((s32[]{:T(128)}, bf16[768,768]{1,0:T(8,128)(2,1)S(1)}, ...), condition=%wide.region_67.68_spmd, body=%wide.region_18.67_spmd.sunk | while | flops 2949123 | bytes 30671168 | solution.py:276
  71.3 3.0 %broadcast_select_fusion.37 = (bf16[768,768]{1,0:T(8,128)(2,1)}, bf16[768,768]{1,0:T(8,128)(2,1)S(1)}, bf16[768,768]{1,0:T(8,128)(2,1)S(1)}) fusion(bf16[768,768]{1,0:T(8,128)(2,1)} %get-tuple-element.935, bf16[768,768]{1,0:T(8,128)(2,1)} %get-tuple-element.936, pred[]{:T(512)} %get-tuple-element.952, pred[]{:T(512)S(6)} %eq.234, ...), kind=kLoop, calls=%fused_computation.25.clone.1 | loop fusion | flops 2359296 | bytes 8257539 | tf_op jit(solution)/shard_map/while/body/eval_jaxpr/jit(_where)/select_n | solution.py:266
  74.2 28.3 %conditional.4 = (bf16[768,768]{1,0:T(8,128)(2,1)}, bf16[768,768]{1,0:T(8,128)(2,1)}) conditional(s32[]{:T(128)} %get-tuple-element.953, (bf16[768,768]{1,0:T(8,128)(2,1)S(1)}, bf16[768,768]{1,0:T(8,128)(2,1)S(1)}) %tuple.272, (bf16[768,768]{1,0:T(8,128)(2,1)S(1)}, bf16[768,768]{1,0:T(8,128)(2,1)S(1)}) %tuple.272, ...), branch_computations={%region_19.19_spmd, %region_20.20_spmd, %region_21.21_spmd, %regio... | conditional | bytes 9437280 | solution.py:269
  74.2 1.7 collective-permute-start.4
  75.9 1.7 collective-permute-start.5
  77.7 24.9 %collective-permute-done.5 = bf16[768,768]{1,0:T(8,128)(2,1)} collective-permute-done((bf16[768,768]{1,0:T(8,128)(2,1)S(1)}, bf16[768,768]{1,0:T(8,128)(2,1)}, u32[]{:S(2)}, u32[]{:S(2)}) %collective-permute-start.5) | collective-permute-done | bytes 1179680 | tf_op jit(solution)/shard_map/while/body/eval_jaxpr/cond/branch_2_fun/ppermute | solution.py:225
  102.5 28.4 %conditional.5 = (bf16[768,768]{1,0:T(8,128)(2,1)}) conditional(s32[]{:T(128)} %get-tuple-element.954, (pred[]{:T(512)}, bf16[768,768]{1,0:T(8,128)(2,1)S(1)}, bf16[768,768]{1,0:T(8,128)(2,1)S(1)}) %tuple.273, (pred[]{:T(512)}, bf16[768,768]{1,0:T(8,128)(2,1)S(1)}, bf16[768,768]{1,0:T(8,128)(2,1)S(1)}) %tuple.273, ...), branch_computations={%region_43.43_spmd, %region_44.44_spmd, %region_45.45_spmd, %regio... | conditional | flops 589824 | bytes 8257585 | solution.py:272
  102.5 0.1 broadcast_select_fusion.19
  102.7 5.2 %collective-permute-start.67 = (bf16[768,768]{1,0:T(8,128)(2,1)S(1)}, bf16[768,768]{1,0:T(8,128)(2,1)}, u32[]{:S(2)}, u32[]{:S(2)}) collective-permute-start(bf16[768,768]{1,0:T(8,128)(2,1)S(1)} %broadcast_select_fusion.19), channel_id=1, source_target_pairs={{0,6},{1,7},{2,0},{3,1},{4,4},{5,5},{6,2},{7,3},{8,14},{9,15},{10,... | collective-permute-start | bytes 3538952 | tf_op jit(solution)/shard_map/while/body/eval_jaxpr/cond/branch_19_fun/ppermute | solution.py:257
  107.8 23.1 %collective-permute-done.67 = bf16[768,768]{1,0:T(8,128)(2,1)} collective-permute-done((bf16[768,768]{1,0:T(8,128)(2,1)S(1)}, bf16[768,768]{1,0:T(8,128)(2,1)}, u32[]{:S(2)}, u32[]{:S(2)}) %collective-permute-start.67) | collective-permute-done | bytes 1179680 | tf_op jit(solution)/shard_map/while/body/eval_jaxpr/cond/branch_19_fun/ppermute | solution.py:257
  130.9 1.3 copy.132
  132.2 0.1 copy.131
  132.3 3.0 %broadcast_select_fusion.37 = (bf16[768,768]{1,0:T(8,128)(2,1)}, bf16[768,768]{1,0:T(8,128)(2,1)S(1)}, bf16[768,768]{1,0:T(8,128)(2,1)S(1)}) fusion(bf16[768,768]{1,0:T(8,128)(2,1)} %get-tuple-element.935, bf16[768,768]{1,0:T(8,128)(2,1)} %get-tuple-element.936, pred[]{:T(512)} %get-tuple-element.952, pred[]{:T(512)S(6)} %eq.234, ...), kind=kLoop, calls=%fused_computation.25.clone.1 | loop fusion | flops 2359296 | bytes 8257539 | tf_op jit(solution)/shard_map/while/body/eval_jaxpr/jit(_where)/select_n | solution.py:266
  135.2 26.2 %conditional.4 = (bf16[768,768]{1,0:T(8,128)(2,1)}, bf16[768,768]{1,0:T(8,128)(2,1)}) conditional(s32[]{:T(128)} %get-tuple-element.953, (bf16[768,768]{1,0:T(8,128)(2,1)S(1)}, bf16[768,768]{1,0:T(8,128)(2,1)S(1)}) %tuple.272, (bf16[768,768]{1,0:T(8,128)(2,1)S(1)}, bf16[768,768]{1,0:T(8,128)(2,1)S(1)}) %tuple.272, ...), branch_computations={%region_19.19_spmd, %region_20.20_spmd, %region_21.21_spmd, %regio... | conditional | bytes 9437280 | solution.py:269
  135.2 1.7 collective-permute-start.4
  136.9 1.5 collective-permute-start.5
  138.4 23.0 %collective-permute-done.5 = bf16[768,768]{1,0:T(8,128)(2,1)} collective-permute-done((bf16[768,768]{1,0:T(8,128)(2,1)S(1)}, bf16[768,768]{1,0:T(8,128)(2,1)}, u32[]{:S(2)}, u32[]{:S(2)}) %collective-permute-start.5) | collective-permute-done | bytes 1179680 | tf_op jit(solution)/shard_map/while/body/eval_jaxpr/cond/branch_2_fun/ppermute | solution.py:225
  161.4 27.1 %conditional.5 = (bf16[768,768]{1,0:T(8,128)(2,1)}) conditional(s32[]{:T(128)} %get-tuple-element.954, (pred[]{:T(512)}, bf16[768,768]{1,0:T(8,128)(2,1)S(1)}, bf16[768,768]{1,0:T(8,128)(2,1)S(1)}) %tuple.273, (pred[]{:T(512)}, bf16[768,768]{1,0:T(8,128)(2,1)S(1)}, bf16[768,768]{1,0:T(8,128)(2,1)S(1)}) %tuple.273, ...), branch_computations={%region_43.43_spmd, %region_44.44_spmd, %region_45.45_spmd, %regio... | conditional | flops 589824 | bytes 8257585 | solution.py:272
  161.4 0.1 broadcast_select_fusion.19
  161.5 6.0 %collective-permute-start.67 = (bf16[768,768]{1,0:T(8,128)(2,1)S(1)}, bf16[768,768]{1,0:T(8,128)(2,1)}, u32[]{:S(2)}, u32[]{:S(2)}) collective-permute-start(bf16[768,768]{1,0:T(8,128)(2,1)S(1)} %broadcast_select_fusion.19), channel_id=1, source_target_pairs={{0,6},{1,7},{2,0},{3,1},{4,4},{5,5},{6,2},{7,3},{8,14},{9,15},{10,... | collective-permute-start | bytes 3538952 | tf_op jit(solution)/shard_map/while/body/eval_jaxpr/cond/branch_19_fun/ppermute | solution.py:257
  167.6 21.0 %collective-permute-done.67 = bf16[768,768]{1,0:T(8,128)(2,1)} collective-permute-done((bf16[768,768]{1,0:T(8,128)(2,1)S(1)}, bf16[768,768]{1,0:T(8,128)(2,1)}, u32[]{:S(2)}, u32[]{:S(2)}) %collective-permute-start.67) | collective-permute-done | bytes 1179680 | tf_op jit(solution)/shard_map/while/body/eval_jaxpr/cond/branch_19_fun/ppermute | solution.py:257
  188.5 1.3 copy.132
  189.9 6.6 %all-to-all-start.2 = ((bf16[1,8,16,1024]{3,2,0,1:T(8,128)(2,1)}), bf16[1,8,16,1024]{3,2,0,1:T(8,128)(2,1)}, u32[]{:S(2)}, u32[]{:S(2)}) async-start(bf16[1,8,16,1024]{3,2,0,1:T(8,128)(2,1)} %bitcast.95), calls=%async_computation.2 | async-start | bytes 524288 | tf_op jit(solution)/shard_map/all_to_all | solution.py:64
  197.1 1.5 broadcast_select_fusion.35
  198.6 6.2 %all-to-all-done.2 = bf16[1,8,16,1024]{3,2,0,1:T(8,128)(2,1)} async-done(((bf16[1,8,16,1024]{3,2,0,1:T(8,128)(2,1)}), bf16[1,8,16,1024]{3,2,0,1:T(8,128)(2,1)}, u32[]{:S(2)}, u32[]{:S(2)}) %all-to-all-start.2) | async-done | bytes 262176 | tf_op jit(solution)/shard_map/all_to_all | solution.py:64
  204.9 0.2 broadcast_select_fusion.29
  205.3 5.4 %maximum_bitcast_fusion.3 = bf16[1,768,1024]{2,1,0:T(8,128)(2,1)} fusion(bf16[128,256]{1,0:T(8,128)(2,1)S(1)} %get-tuple-element.783, bf16[128,256]{1,0:T(8,128)(2,1)S(1)} %get-tuple-element.784, bf16[128,256]{1,0:T(8,128)(2,1)S(1)} %get-tuple-element.782, bf16[384,768]{1,0:T(8,128)(2,1)S(1)} %slice.188, bf16[128,256]{1,0:T(8,128)(2,1)S(1)} %get-tuple-element.780, ...), kind=kLoop, calls=%fused_computation.60 | loop fusion | flops 12582912 | bytes 3145728 | tf_op jit(solution)/shard_map/broadcast_in_dim | solution.py:182
  210.7 2.1 fusion.31
  212.8 14.2 %collective-permute-done.73 = bf16[768,768]{1,0:T(8,128)(2,1)S(1)} collective-permute-done((bf16[768,768]{1,0:T(8,128)(2,1)S(1)}, bf16[768,768]{1,0:T(8,128)(2,1)S(1)}, u32[]{:S(2)}, u32[]{:S(2)}) %collective-permute-start.73) | collective-permute-done | bytes 1179680 | tf_op jit(solution)/shard_map/ppermute | solution.py:225
  226.9 1.6 broadcast_select_fusion.28
  228.5 0.1 maximum_bitcast_fusion.1
  228.6 0.1 maximum_bitcast_fusion.2
  228.7 1.9 maximum_bitcast_fusion
  (49 shorter events, 0.8 us)
Async XLA Ops:
  0.6 0.9 copy-start
  1.4 16.4 %copy-start.8 = (pred[8,16]{1,0:T(8,128)(4,1)}, pred[8,16]{1,0:T(8,128)(4,1)S(1)}, u32[]{:S(2)}) copy-start(pred[8,16]{1,0:T(8,128)(4,1)S(1)} %compare_bitcast_fusion) | copy-start | bytes 388
  1.6 16.3 %copy-start.4 = (s32[8,16]{1,0:T(8,128)}, s32[8,16]{1,0:T(8,128)S(1)}, u32[]{:S(2)}) copy-start(s32[8,16]{1,0:T(8,128)S(1)} %copy.40) | copy-start | bytes 1540
  2.6 31.4 %all-to-all-start = ((bf16[1,8,16,1024]{3,2,0,1:T(8,128)(2,1)}), bf16[1,8,16,1024]{3,2,0,1:T(8,128)(2,1)}, u32[]{:S(2)}, u32[]{:S(2)}) async-start(bf16[1,8,16,1024]{3,2,0,1:T(8,128)(2,1)} %fusion.29), calls=%async_computation | async-start | bytes 524288 | tf_op jit(solution)/shard_map/all_to_all | solution.py:64
  17.9 0.7 copy-start.7
  17.9 0.8 copy-start.11
  41.0 5.7 %copy-start.2 = (bf16[2,768,768]{2,1,0:T(8,128)(2,1)}, bf16[2,768,768]{2,1,0:T(8,128)(2,1)S(1)}, u32[]{:S(2)}) copy-start(bf16[2,768,768]{2,1,0:T(8,128)(2,1)S(1)} %fusion.9) | copy-start | bytes 7077892
  42.4 27.7 %collective-permute-start.72 = (bf16[768,768]{1,0:T(8,128)(2,1)}, bf16[768,768]{1,0:T(8,128)(2,1)S(1)}, u32[]{:S(2)}, u32[]{:S(2)}) collective-permute-start(bf16[768,768]{1,0:T(8,128)(2,1)} %broadcast_select_fusion.32), channel_id=1, source_target_pairs={{0,1},{1,0},{2,3},{3,2},{4,5},{5,4},{6,7},{7,6},{8,9},{9,8},{10,11... | collective-permute-start | bytes 3538952 | tf_op jit(solution)/shard_map/ppermute | solution.py:225
  46.7 11.6 %all-to-all-start.1 = ((bf16[1,4,32,1536]{3,2,0,1:T(8,128)(2,1)}), bf16[1,4,32,1536]{3,2,0,1:T(8,128)(2,1)}, u32[]{:S(2)}, u32[]{:S(2)}) async-start(bf16[1,4,32,1536]{3,2,0,1:T(8,128)(2,1)} %bitcast.28), calls=%async_computation.1 | async-start | bytes 786432 | tf_op jit(solution)/shard_map/all_to_all | solution.py:42
  71.2 125.8 %copy-start.6 = (s32[1,16,8]{1,2,0:T(8,128)S(1)}, s32[1,16,8]{1,2,0:T(8,128)}, u32[]{:S(2)}) copy-start(s32[1,16,8]{1,2,0:T(8,128)} %param.71) | copy-start | bytes 1540
  71.3 125.8 %copy-start.10 = (f32[1,16,8]{1,2,0:T(8,128)S(1)}, f32[1,16,8]{1,2,0:T(8,128)}, u32[]{:S(2)}) copy-start(f32[1,16,8]{1,2,0:T(8,128)} %param.72) | copy-start | bytes 1540
  74.2 3.4 %collective-permute-start.4 = (bf16[768,768]{1,0:T(8,128)(2,1)S(1)}, bf16[768,768]{1,0:T(8,128)(2,1)}, u32[]{:S(2)}, u32[]{:S(2)}) collective-permute-start(bf16[768,768]{1,0:T(8,128)(2,1)S(1)} %get-tuple-element.572), channel_id=1, source_target_pairs={{0,0},{1,1},{2,4},{3,5},{4,2},{5,3},{6,6},{7,7},{8,8},{9,9},{10,12... | collective-permute-start | bytes 3538952 | tf_op jit(solution)/shard_map/while/body/eval_jaxpr/cond/branch_2_fun/ppermute | solution.py:257
  75.9 26.6 %collective-permute-start.5 = (bf16[768,768]{1,0:T(8,128)(2,1)S(1)}, bf16[768,768]{1,0:T(8,128)(2,1)}, u32[]{:S(2)}, u32[]{:S(2)}) collective-permute-start(bf16[768,768]{1,0:T(8,128)(2,1)S(1)} %get-tuple-element.573), channel_id=1, source_target_pairs={{0,1},{1,0},{2,3},{3,2},{4,5},{5,4},{6,7},{7,6},{8,9},{9,8},{10,11... | collective-permute-start | bytes 3538952 | tf_op jit(solution)/shard_map/while/body/eval_jaxpr/cond/branch_2_fun/ppermute | solution.py:225
  102.7 28.2 %collective-permute-start.67 = (bf16[768,768]{1,0:T(8,128)(2,1)S(1)}, bf16[768,768]{1,0:T(8,128)(2,1)}, u32[]{:S(2)}, u32[]{:S(2)}) collective-permute-start(bf16[768,768]{1,0:T(8,128)(2,1)S(1)} %broadcast_select_fusion.19), channel_id=1, source_target_pairs={{0,6},{1,7},{2,0},{3,1},{4,4},{5,5},{6,2},{7,3},{8,14},{9,15},{10,... | collective-permute-start | bytes 3538952 | tf_op jit(solution)/shard_map/while/body/eval_jaxpr/cond/branch_19_fun/ppermute | solution.py:257
  135.2 3.1 %collective-permute-start.4 = (bf16[768,768]{1,0:T(8,128)(2,1)S(1)}, bf16[768,768]{1,0:T(8,128)(2,1)}, u32[]{:S(2)}, u32[]{:S(2)}) collective-permute-start(bf16[768,768]{1,0:T(8,128)(2,1)S(1)} %get-tuple-element.572), channel_id=1, source_target_pairs={{0,0},{1,1},{2,4},{3,5},{4,2},{5,3},{6,6},{7,7},{8,8},{9,9},{10,12... | collective-permute-start | bytes 3538952 | tf_op jit(solution)/shard_map/while/body/eval_jaxpr/cond/branch_2_fun/ppermute | solution.py:257
  136.9 24.5 %collective-permute-start.5 = (bf16[768,768]{1,0:T(8,128)(2,1)S(1)}, bf16[768,768]{1,0:T(8,128)(2,1)}, u32[]{:S(2)}, u32[]{:S(2)}) collective-permute-start(bf16[768,768]{1,0:T(8,128)(2,1)S(1)} %get-tuple-element.573), channel_id=1, source_target_pairs={{0,1},{1,0},{2,3},{3,2},{4,5},{5,4},{6,7},{7,6},{8,9},{9,8},{10,11... | collective-permute-start | bytes 3538952 | tf_op jit(solution)/shard_map/while/body/eval_jaxpr/cond/branch_2_fun/ppermute | solution.py:225
  161.5 27.0 %collective-permute-start.67 = (bf16[768,768]{1,0:T(8,128)(2,1)S(1)}, bf16[768,768]{1,0:T(8,128)(2,1)}, u32[]{:S(2)}, u32[]{:S(2)}) collective-permute-start(bf16[768,768]{1,0:T(8,128)(2,1)S(1)} %broadcast_select_fusion.19), channel_id=1, source_target_pairs={{0,6},{1,7},{2,0},{3,1},{4,4},{5,5},{6,2},{7,3},{8,14},{9,15},{10,... | collective-permute-start | bytes 3538952 | tf_op jit(solution)/shard_map/while/body/eval_jaxpr/cond/branch_19_fun/ppermute | solution.py:257
  189.9 15.0 %all-to-all-start.2 = ((bf16[1,8,16,1024]{3,2,0,1:T(8,128)(2,1)}), bf16[1,8,16,1024]{3,2,0,1:T(8,128)(2,1)}, u32[]{:S(2)}, u32[]{:S(2)}) async-start(bf16[1,8,16,1024]{3,2,0,1:T(8,128)(2,1)} %bitcast.95), calls=%async_computation.2 | async-start | bytes 524288 | tf_op jit(solution)/shard_map/all_to_all | solution.py:64
  197.1 7.8 %copy-start.3 = (bf16[768,768]{1,0:T(8,128)(2,1)S(1)}, bf16[768,768]{1,0:T(8,128)(2,1)}, u32[]{:S(2)}) copy-start(bf16[768,768]{1,0:T(8,128)(2,1)} %get-tuple-element.733) | copy-start | bytes 3538948
  204.9 22.1 %collective-permute-start.73 = (bf16[768,768]{1,0:T(8,128)(2,1)S(1)}, bf16[768,768]{1,0:T(8,128)(2,1)S(1)}, u32[]{:S(2)}, u32[]{:S(2)}) collective-permute-start(bf16[768,768]{1,0:T(8,128)(2,1)S(1)} %broadcast_select_fusion.35), channel_id=1, source_target_pairs={{0,1},{1,0},{2,3},{3,2},{4,5},{5,4},{6,7},{7,6},{8,9},{9,8},{10,11... | collective-permute-start | bytes 3538952 | tf_op jit(solution)/shard_map/ppermute | solution.py:225
  205.3 5.4 %copy-start.5 = (s32[8,16]{1,0:T(8,128)S(1)}, s32[8,16]{1,0:T(8,128)}, u32[]{:S(2)}) copy-start(s32[8,16]{1,0:T(8,128)} %copy-done.4) | copy-start | bytes 1540
  205.3 5.4 %copy-start.9 = (pred[8,16]{1,0:T(8,128)(4,1)S(1)}, pred[8,16]{1,0:T(8,128)(4,1)}, u32[]{:S(2)}) copy-start(pred[8,16]{1,0:T(8,128)(4,1)} %copy-done.8) | copy-start | bytes 388
  228.7 2.0 copy-start.1
